TPU v7x, 32 devices: a whole 2x2x4 slice. The times are simulated.
32 devices in a mesh: region: 16 (over z, y, x), mp: 2 (over core).
Axes of the slice: x: 2, y: 2, z: 4, core: 2. Of those that a mesh axis runs over, the one named last changes fastest.
Arguments:
- tokens: bfloat16 [16384, 1024], P('region')
- ln_gain: bfloat16 [1024], replicated, may hold values from 0.25 to 1.75
- w_qkv: bfloat16 [1024, 3, 1024], P(None, None, 'mp')
- w_out: bfloat16 [1024, 1024], P('mp'), may hold values from -0.75 to 0.75
- neighbours: int32 [256, 8], P('region'), may hold values from 0 to 255, as said below
- degree: int32 [256], P('region'), may hold values from 1 to 8
Outputs:
- update: bfloat16 [16384, 1024], P('region')
Inputs may be any that keep to these rules, and one draw needn't show every extreme that they name: A neighbour of a patch with local index below 2 in its region (local index = id % 16, region = id // 16) lies in the same region or is one of the last 2 patches of region r-1 or r-2 (cyclically); of local index 14 or more: same region or one of the first 2 patches of region r+1 or r+2; any other patch's neighbours lie in its own region. Only the first degree[p] entries of a row count.
All inputs are finite; a program needn't handle non-finite values.
Results may differ from a plain program's by a relative error of at most 0.012.
The roundings to bfloat16 on the way count: a program that leaves them out, or rounds other values in their place, can miss the bound.
Values may be sent and summed in bfloat16 or wider, within the bound.
A program may use at most 192 MiB of HBM per device.

v0:
```python
import jax
import jax.numpy as jnp
from jax import lax
from jax.sharding import PartitionSpec as P

HDIM = 64
NBR = 8
RIM = 2


def spread_2(value, axis, source):
    kept = jnp.where(lax.axis_index(axis) == source, value, 0).astype(value.dtype)
    return lax.psum(kept, axis)


def from_behind(block, axis, distance):
    devices = range(lax.axis_size(axis))
    route = [((i - distance) % len(devices), i) for i in devices]
    return lax.ppermute(block, axis, route)


def layer_norm(rows, gain):
    values = rows.astype(jnp.float32)
    centre = jnp.mean(values, axis=-1, keepdims=True)
    spread = jnp.mean((values - centre) ** 2, axis=-1, keepdims=True)
    return ((values - centre) * lax.rsqrt(spread + 1e-05) * gain.astype(jnp.float32)).astype(
        jnp.bfloat16
    )


def project(block, w_flat, feat):
    out = jnp.dot(block, w_flat, preferred_element_type=jnp.float32).reshape(-1, 3, feat)
    query = (out[:, 0, :] * (1.0 / HDIM**0.5)).astype(jnp.bfloat16)
    pair = jnp.stack([out[:, 1, :].astype(jnp.bfloat16), out[:, 2, :].astype(jnp.bfloat16)], axis=1)
    return (query, pair)


def attend_block(query, pairs, valid, heads):
    npat, keys = (pairs.shape[0], pairs.shape[1])
    patch = query.shape[1]
    query = query.reshape(npat, patch, heads, HDIM)
    key_part = pairs[:, :, 0, :].reshape(npat, keys, heads, HDIM)
    value_part = pairs[:, :, 1, :].reshape(npat, keys, heads, HDIM)
    scores = jnp.einsum("pqhd,pkhd->phqk", query, key_part, preferred_element_type=jnp.float32)
    scores = jnp.where(valid[:, None, None, :], scores, jnp.float32(-1e30))
    top = jnp.max(scores, axis=-1, keepdims=True)
    expo = jnp.exp(scores - top)
    total = jnp.sum(expo, axis=-1)
    weights = expo.astype(jnp.bfloat16)
    context = jnp.einsum("phqk,pkhd->pqhd", weights, value_part, preferred_element_type=jnp.float32)
    context = context / jnp.transpose(total, (0, 2, 1))[..., None]
    return context.astype(jnp.bfloat16).reshape(npat * patch, heads * HDIM)


def per_device(tokens, ln_gain, w_qkv, w_out, neighbours, degree):
    rows, width = tokens.shape
    npat = neighbours.shape[0]
    patch = rows // npat
    feat = w_qkv.shape[2]
    heads_here = feat // HDIM
    rim = RIM
    normed = layer_norm(tokens, ln_gain)
    w_flat = w_qkv.reshape(width, 3 * feat)
    query, pairs = project(normed, w_flat, feat)
    kv_pat = pairs.reshape(npat, patch, 2, feat)
    anchor = spread_2(kv_pat[0], "region", 0)

    def fetch_before(step):
        return from_behind(kv_pat[npat - rim :], "region", step)

    def fetch_after(step):
        return from_behind(kv_pat[:rim], "region", step)

    table = jnp.concatenate(
        [kv_pat, fetch_before(1), fetch_before(2), fetch_after(-1), fetch_after(-2)], axis=0
    )
    cycle = lax.axis_size("region")
    region_id = lax.axis_index("region")
    owner = neighbours // npat
    local = neighbours % npat
    reach = (owner - region_id) % cycle
    slot = jnp.where(
        reach == 0,
        local,
        jnp.where(
            reach == cycle - 1,
            npat + local - (npat - rim),
            jnp.where(
                reach == cycle - 2,
                npat + rim + local - (npat - rim),
                jnp.where(reach == 1, npat + 2 * rim + local, npat + 3 * rim + local),
            ),
        ),
    )
    far = table[slot].reshape(npat, NBR * patch, 2, feat)
    anchors = jnp.broadcast_to(anchor[None], (npat, patch, 2, feat))
    keyed = jnp.concatenate([kv_pat, far, anchors], axis=1)
    slot_ok = jnp.arange(NBR, dtype=jnp.int32)[None, :] < degree[:, None]
    far_ok = jnp.repeat(slot_ok, patch, axis=1)
    ones = jnp.ones((npat, patch), dtype=bool)
    valid = jnp.concatenate([ones, far_ok, ones], axis=1)
    context = attend_block(query.reshape(npat, patch, feat), keyed, valid, heads_here)
    partial_sum = jnp.dot(context, w_out, preferred_element_type=jnp.float32)
    return lax.psum(partial_sum, "mp").astype(jnp.bfloat16)


def solution(mesh):
    placed = (
        P("region", None),
        P(),
        P(None, None, "mp"),
        P("mp", None),
        P("region", None),
        P("region"),
    )
    return jax.shard_map(
        per_device, mesh=mesh, in_specs=placed, out_specs=P("region", None), check_vma=False
    )
```

profile of v0, /device:TPU:0, one launch (start us, length us, event | category | flops | bytes accessed | tf_op | source)
XLA Modules:
  0.0 281.2 jit_solution(11935173775363583606)
XLA Ops:
  6.5 0.0 all-reduce.3.cloned.1.call-start
  6.5 0.8 convert_element_type.32
  7.3 1.9 convert_reduce_fusion
  9.3 0.0 copy-start.3
  9.3 2.4 fusion.9
  11.7 4.7 %copy.11 = bf16[1024,3,512]{0,2,1:T(8,128)(2,1)} copy(bf16[1024,3,512]{2,0,1:T(8,128)(2,1)} %param.8) | data formatting | bytes 6291456 | tf_op args[2]
  16.4 7.5 %fusion.32 = (bf16[1024,3,512]{2,0,1:T(8,128)(2,1)S(1)}, f32[1024,3,512]{2,0,1:T(8,128)}) fusion(bf16[1024,3,512]{0,2,1:T(8,128)(2,1)} %copy.11, bf16[1024,1024]{1,0:T(8,128)(2,1)S(1)} %copy-done.3, f32[1024]{0:T(1024)S(1)} %convert_element_type.32, f32[1024]{0:T(1024)S(1)} %add_rsqrt_fusion, f32[1024]{0:T(1024)S(1)} %broadcast_multiply_fusion), kind=kOutput, calls=%fused_computation.57 | convolution fusion | flops 3228041216 | bytes 14692352 | tf_op jit(solution)/shard_map/dot_general | solution.py:32
  23.9 1.7 copy-done.4
  25.6 0.9 fusion.30
  26.5 3.0 %collective-permute-start.1 = (bf16[2,64,2,512]{3,1,0,2:T(8,128)(2,1)}, bf16[2,64,2,512]{3,1,0,2:T(8,128)(2,1)}, u32[]{:S(2)}, u32[]{:S(2)}) collective-permute-start(bf16[2,64,2,512]{3,1,0,2:T(8,128)(2,1)} %bitcast.6), channel_id=1, source_target_pairs={{28,0},{30,2},{0,4},{2,6},{4,8},{6,10},{8,12},{10,14},{12,16},{14,... | collective-permute-start | bytes 786440 | tf_op jit(solution)/shard_map/ppermute | solution.py:19
  29.5 1.5 collective-permute-start
  30.9 3.2 %collective-permute-start.3 = (bf16[2,64,2,512]{3,1,0,2:T(8,128)(2,1)}, bf16[2,64,2,512]{3,1,0,2:T(8,128)(2,1)S(1)}, u32[]{:S(2)}, u32[]{:S(2)}) collective-permute-start(bf16[2,64,2,512]{3,1,0,2:T(8,128)(2,1)} %bitcast.7), channel_id=1, source_target_pairs={{4,0},{6,2},{8,4},{10,6},{12,8},{14,10},{16,12},{18,14},{20,16},{2... | collective-permute-start | bytes 786440 | tf_op jit(solution)/shard_map/ppermute | solution.py:19
  34.1 1.3 collective-permute-start.2
  35.4 1.6 slice_select_fusion
  37.0 0.0 all-reduce.3.cloned.1.call-update
  37.0 1.7 fusion.31
  38.8 0.1 iota_compare_fusion
  38.9 3.5 %fusion.19 = bf16[1024,1,512]{2,0,1:T(8,128)(2,1)} fusion(f32[1024,3,512]{2,0,1:T(8,128)} %get-tuple-element.12), kind=kLoop, calls=%fused_computation.23 | loop fusion | flops 1048576 | bytes 3145728 | tf_op jit(solution)/shard_map/convert_element_type | solution.py:33
  42.3 1.5 maximum_dynamic-update-slice_fusion
  43.9 0.1 broadcast_in_dim.43
  43.9 0.1 reshape.45
  44.1 0.1 pad_add_fusion
  44.1 0.1 copy.12
  44.2 0.1 reshape.49
  44.3 3.0 %convert_element_type.35 = bf16[16,64,8,64]{3,2,1,0:T(8,128)(2,1)S(1)} reshape(bf16[1024,1,512]{2,0,1:T(8,128)(2,1)} %fusion.19) | data formatting | bytes 2097152 | tf_op jit(solution)/shard_map/convert_element_type | solution.py:33
  47.3 0.0 collective-permute-done
  47.3 1.7 constant_dynamic-update-slice_fusion.3
  49.0 0.0 collective-permute-done.1
  49.0 1.7 constant_dynamic-update-slice_fusion.2
  50.7 0.0 collective-permute-done.2
  50.7 1.7 constant_dynamic-update-slice_fusion.1
  52.4 0.0 collective-permute-done.3
  52.4 0.7 constant_dynamic-update-slice_fusion
  53.1 10.2 %gather_fusion = bf16[128,64,2,512]{3,1,2,0:T(8,128)(2,1)} fusion(bf16[24,64,2,512]{3,1,0,2:T(8,128)(2,1)} %constant_dynamic-update-slice_fusion, s32[1024]{0:T(1024)S(1)} %pad_clamp_fusion), kind=kCustom, calls=%fused_computation | custom fusion | bytes 33554944 | tf_op jit(solution)/shard_map/gather | solution.py:95
  63.3 14.1 %copy.13 = bf16[128,64,2,512]{3,1,0,2:T(8,128)(2,1)} copy(bf16[128,64,2,512]{3,1,2,0:T(8,128)(2,1)} %gather_fusion) | data formatting | bytes 33554432 | tf_op jit(solution)/shard_map/gather | solution.py:95
  77.4 65.8 %all-reduce.3.cloned.1.call-done = bf16[64,2,512]{2,0,1:T(8,128)(2,1)} async-done(((bf16[64,2,512]{2,0,1:T(8,128)(2,1)}), bf16[64,2,512]{2,0,1:T(8,128)(2,1)}) %all-reduce.3.cloned.1.call-update) | async-done | bytes 131088 | tf_op jit(solution)/shard_map/psum | solution.py:13
  143.1 2.5 broadcast_in_dim.41
  145.6 21.4 %pad_maximum_fusion = bf16[16,640,2,512]{3,1,0,2:T(8,128)(2,1)} fusion(bf16[16,64,2,512]{3,1,0,2:T(8,128)(2,1)} %broadcast_in_dim.41, bf16[16,512,2,512]{3,1,0,2:T(8,128)(2,1)} %bitcast.35, bf16[16,64,1,512]{3,1,0,2:T(8,128)(2,1)} %bitcast.40, bf16[16,64,1,512]{3,1,0,2:T(8,128)(2,1)} %bitcast.38), kind=kLoop, calls=%fused_computation.1 | loop fusion | flops 83886080 | bytes 41943040 | tf_op jit(solution)/shard_map/concatenate | solution.py:97
  167.0 16.1 %fusion.29 = (bf16[16,640,1,512]{3,1,0,2:T(8,128)(2,1)}, bf16[16,640,1,512]{3,1,0,2:T(8,128)(2,1)}) fusion(bf16[16,640,2,512]{3,1,0,2:T(8,128)(2,1)} %pad_maximum_fusion), kind=kLoop, calls=%fused_computation.54 | loop fusion | bytes 41943040 | tf_op jit(solution)/shard_map/slice | solution.py:42
  183.1 15.0 %copy.15 = bf16[16,640,1,512]{1,3,0,2:T(8,128)(2,1)} copy(bf16[16,640,1,512]{3,1,0,2:T(8,128)(2,1)} %get-tuple-element.5) | data formatting | bytes 20971520 | tf_op jit(solution)/shard_map/slice | solution.py:42
  198.1 14.5 %copy.14 = bf16[16,640,1,512]{1,3,0,2:T(8,128)(2,1)} copy(bf16[16,640,1,512]{3,1,0,2:T(8,128)(2,1)} %get-tuple-element.6) | data formatting | bytes 20971520 | tf_op jit(solution)/shard_map/slice | solution.py:43
  212.7 13.9 %select_reduce_fusion = (f32[16,8,64]{2,1,0:T(8,128)S(1)}, f32[16,8,64,640]{3,2,1,0:T(8,128)}) fusion(pred[16,640]{1,0:T(8,128)(4,1)S(1)} %pad_add_fusion, bf16[16,640,8,64]{1,3,2,0:T(8,128)(2,1)} %bitcast.34, bf16[16,64,8,64]{3,2,1,0:T(8,128)(2,1)S(1)} %convert_element_type.35), kind=kOutput, calls=%fused_computation.3 | convolution fusion | flops 681566208 | bytes 32548864 | tf_op jit(solution)/shard_map/pqhd,pkhd->phqk/dot_general | solution.py:44
  226.5 9.4 %fusion = f32[16,8,64]{2,1,0:T(8,128)S(1)} fusion(f32[16,8,64,640]{3,2,1,0:T(8,128)} %get-tuple-element.14, f32[16,8,64]{2,1,0:T(8,128)S(1)} %get-tuple-element.13, pred[16,640]{1,0:T(8,128)(4,1)S(1)} %pad_add_fusion), kind=kLoop, calls=%fused_computation.4 | loop fusion | flops 15720448 | bytes 21047296 | tf_op jit(solution)/shard_map/reduce_sum | solution.py:48
  236.0 13.5 %fusion.12 = bf16[16,64,8,64]{1,3,2,0:T(8,128)(2,1)} fusion(bf16[16,640,8,64]{1,3,2,0:T(8,128)(2,1)} %bitcast.36, f32[16,8,64,640]{3,2,1,0:T(8,128)} %get-tuple-element.14, f32[16,8,64]{2,1,0:T(8,128)S(1)} %get-tuple-element.13, pred[16,640]{1,0:T(8,128)(4,1)S(1)} %pad_add_fusion, f32[16,64,8]{1,2,0:T(8,128)S(1)} %bitcast.41), kind=kOutput, calls=%fused_computation.18 | convolution fusion | flops 687865856 | bytes 32581632 | tf_op jit(solution)/shard_map/phqk,pkhd->pqhd/dot_general | solution.py:50
  249.5 3.2 %copy.17 = bf16[16,64,8,64]{3,2,1,0:T(8,128)(2,1)S(1)} copy(bf16[16,64,8,64]{1,3,2,0:T(8,128)(2,1)} %fusion.12) | data formatting | bytes 2097152 | tf_op jit(solution)/shard_map/convert_element_type | solution.py:52
  252.8 2.0 reshape.46
  254.8 4.4 %fusion.33 = f32[1024,1024]{1,0:T(8,128)} fusion(bf16[1024,512]{1,0:T(8,128)(2,1)} %reshape.46, bf16[512,1024]{1,0:T(8,128)(2,1)S(1)} %copy-done), kind=kOutput, calls=%fused_computation.58 | convolution fusion | flops 1073741824 | bytes 6291456 | tf_op jit(solution)/shard_map/dot_general | solution.py:103
  259.2 15.1 %all-reduce.4 = bf16[1024,1024]{1,0:T(8,128)(2,1)} all-reduce(f32[1024,1024]{1,0:T(8,128)} %fusion.33), channel_id=1, replica_groups=mesh['region'=16,'mp'=2] {'mp'}, use_global_device_ids=true, to_apply=%region_5.6 | all-reduce | flops 1048576 | bytes 6291456 | tf_op jit(solution)/shard_map/psum | solution.py:104
  (17 shorter events, 0.1 us)
Async XLA Ops:
  6.5 248.3 %copy-start = (bf16[512,1024]{1,0:T(8,128)(2,1)S(1)}, bf16[512,1024]{1,0:T(8,128)(2,1)}, u32[]{:S(2)}) copy-start(bf16[512,1024]{1,0:T(8,128)(2,1)} %param.9) | copy-start | bytes 3145732
  6.5 136.6 %all-reduce.3.cloned.1.call-start = ((), (), s32[]{:S(2)}) async-start(), calls=%async_computation | async-start | bytes 262144 | tf_op jit(solution)/shard_map/psum | solution.py:13
  9.3 7.1 %copy-start.3 = (bf16[1024,1024]{1,0:T(8,128)(2,1)S(1)}, bf16[1024,1024]{1,0:T(8,128)(2,1)}, u32[]{:S(2)}) copy-start(bf16[1024,1024]{1,0:T(8,128)(2,1)} %param.6) | copy-start | bytes 6291460
  23.9 1.7 copy-start.4
  23.9 14.8 %copy-start.6 = (s32[16]{0:T(128)S(1)}, s32[16]{0:T(128)}, u32[]{:S(2)}) copy-start(s32[16]{0:T(128)} %param.11) | copy-start | bytes 196
  23.9 14.9 %copy-start.5 = (s32[16,8]{0,1:T(8,128)S(1)}, s32[16,8]{0,1:T(8,128)}, u32[]{:S(2)}) copy-start(s32[16,8]{0,1:T(8,128)} %param.10) | copy-start | bytes 1540
  26.5 22.5 %collective-permute-start.1 = (bf16[2,64,2,512]{3,1,0,2:T(8,128)(2,1)}, bf16[2,64,2,512]{3,1,0,2:T(8,128)(2,1)}, u32[]{:S(2)}, u32[]{:S(2)}) collective-permute-start(bf16[2,64,2,512]{3,1,0,2:T(8,128)(2,1)} %bitcast.6), channel_id=1, source_target_pairs={{28,0},{30,2},{0,4},{2,6},{4,8},{6,10},{8,12},{10,14},{12,16},{14,... | collective-permute-start | bytes 786440 | tf_op jit(solution)/shard_map/ppermute | solution.py:19
  29.5 17.8 %collective-permute-start = (bf16[2,64,2,512]{3,1,0,2:T(8,128)(2,1)}, bf16[2,64,2,512]{3,1,0,2:T(8,128)(2,1)}, u32[]{:S(2)}, u32[]{:S(2)}) collective-permute-start(bf16[2,64,2,512]{3,1,0,2:T(8,128)(2,1)} %bitcast.6), channel_id=1, source_target_pairs={{30,0},{0,2},{2,4},{4,6},{6,8},{8,10},{10,12},{12,14},{14,16},{16,... | collective-permute-start | bytes 786440 | tf_op jit(solution)/shard_map/ppermute | solution.py:19
  30.9 21.4 %collective-permute-start.3 = (bf16[2,64,2,512]{3,1,0,2:T(8,128)(2,1)}, bf16[2,64,2,512]{3,1,0,2:T(8,128)(2,1)S(1)}, u32[]{:S(2)}, u32[]{:S(2)}) collective-permute-start(bf16[2,64,2,512]{3,1,0,2:T(8,128)(2,1)} %bitcast.7), channel_id=1, source_target_pairs={{4,0},{6,2},{8,4},{10,6},{12,8},{14,10},{16,12},{18,14},{20,16},{2... | collective-permute-start | bytes 786440 | tf_op jit(solution)/shard_map/ppermute | solution.py:19
  34.1 16.5 %collective-permute-start.2 = (bf16[2,64,2,512]{3,1,0,2:T(8,128)(2,1)}, bf16[2,64,2,512]{3,1,0,2:T(8,128)(2,1)}, u32[]{:S(2)}, u32[]{:S(2)}) collective-permute-start(bf16[2,64,2,512]{3,1,0,2:T(8,128)(2,1)} %bitcast.7), channel_id=1, source_target_pairs={{2,0},{4,2},{6,4},{8,6},{10,8},{12,10},{14,12},{16,14},{18,16},{20... | collective-permute-start | bytes 786440 | tf_op jit(solution)/shard_map/ppermute | solution.py:19
  38.7 3.6 %copy-start.1 = (bf16[1024,1,512]{2,0,1:T(8,128)(2,1)}, bf16[1024,1,512]{2,0,1:T(8,128)(2,1)S(1)}, u32[]{:S(2)}) copy-start(bf16[1024,1,512]{2,0,1:T(8,128)(2,1)S(1)} %get-tuple-element.9) | copy-start | bytes 3145732
  38.7 5.1 %copy-start.2 = (bf16[1024,1,512]{2,0,1:T(8,128)(2,1)}, bf16[1024,1,512]{2,0,1:T(8,128)(2,1)S(1)}, u32[]{:S(2)}) copy-start(bf16[1024,1,512]{2,0,1:T(8,128)(2,1)S(1)} %get-tuple-element.10) | copy-start | bytes 3145732
Sparse Core Ops, SparseCore 0:
  37.2 105.9 all-reduce.2
where the time goes:
time: 283 us; the launch traced here: 281 us
  local copies, waits for them, and re-layouts  95.8 us (34%)
  waiting for transfers between devices  65.8 us (23%)
  other arithmetic  42.7 us (15%)
  matrix products  39.3 us (14%)
  blocking collectives  15.1 us (5%)
  between operations  13.5 us (5%)
  starting transfers between devices  8.96 us (3%)
    psum x1, waiting for transfers between devices, spread_2(): return lax.psum(kept, axis)  65.8 us
    slice x2, local copies, waits for them, and re-layouts, attend_block(): key_part = pairs[:, :, 0, :].reshape(npat, keys, heads, HDIM)  31.2 us
    gather x2, local copies, waits for them, and re-layouts, per_device(): far = table[slot].reshape(npat, NBR * patch, 2, feat)  24.3 us
    concatenate x1, other arithmetic, per_device(): keyed = jnp.concatenate([kv_pat, far, anchors], axis=1)  21.4 us
    psum x1, blocking collectives, per_device(): return lax.psum(partial_sum, 'mp').astype(jnp.bfloat16)  15.1 us
    slice x1, local copies, waits for them, and re-layouts, attend_block(): value_part = pairs[:, :, 1, :].reshape(npat, keys, heads, HDIM)  14.5 us
    dot_general x1, matrix products, attend_block(): jnp.einsum('pqhd,pkhd->phqk', query, key_part, preferred_element_type=jnp...  13.9 us
    dot_general x1, matrix products, attend_block(): jnp.einsum('phqk,pkhd->pqhd', weights, value_part, preferred_element_type...  13.5 us
  transfers between devices with their start and end apart: 5, of which 1 were waited for; matrix products, arithmetic and copies ran while one was open for 15% of the time, Pallas kernels for 0%

commit v1 on v0

--- a/solution.py
+++ b/solution.py
@@ -101,7 +101,8 @@
     valid = jnp.concatenate([ones, far_ok, ones], axis=1)
     context = attend_block(query.reshape(npat, patch, feat), keyed, valid, heads_here)
     partial_sum = jnp.dot(context, w_out, preferred_element_type=jnp.float32)
-    return lax.psum(partial_sum, "mp").astype(jnp.bfloat16)
+    rows_solve = lambda base_x: jnp.sum(lax.all_gather(base_x, "mp"), axis=0)
+    return rows_solve(partial_sum).astype(jnp.bfloat16)
 
 
 def solution(mesh):

time: 283 us -> 293 us (1.035)
  waiting for transfers between devices: 65.8 us -> 84.8 us
  blocking collectives: 15.1 us -> 0 us
  other arithmetic: 42.7 us -> 48.9 us
    all_gather x0 -> x1, waiting for transfers between devices: none -> 19.1 us  [per_device(): rows_solve = lambda base_x: jnp.sum(lax.all_gather(base_x, 'mp'), axis=0)]
    psum x1 -> x0, blocking collectives: 15.1 us -> none  [per_device(): return lax.psum(partial_sum, 'mp').astype(jnp.bfloat16)]
    reduce_sum x0 -> x1, other arithmetic: none -> 6.23 us  [per_device(): rows_solve = lambda base_x: jnp.sum(lax.all_gather(base_x, 'mp'), axis=0)]
  transfers between devices with their start and end apart: 5 -> 6, of which waited for: 1 -> 2; matrix products, arithmetic and copies ran while one was open for 15% -> 14% of each run, Pallas kernels for 0% -> 0%
where the time goes in v1:
time: 293 us; the launch traced here: 292 us
  local copies, waits for them, and re-layouts  96.1 us (33%)
  waiting for transfers between devices  84.8 us (29%)
  other arithmetic  48.9 us (17%)
  matrix products  39.4 us (13%)
  between operations  13.5 us (5%)
  starting transfers between devices  9.01 us (3%)
    psum x1, waiting for transfers between devices, spread_2(): return lax.psum(kept, axis)  65.7 us
    slice x2, local copies, waits for them, and re-layouts, attend_block(): key_part = pairs[:, :, 0, :].reshape(npat, keys, heads, HDIM)  30.9 us
    gather x2, local copies, waits for them, and re-layouts, per_device(): far = table[slot].reshape(npat, NBR * patch, 2, feat)  24.3 us
    concatenate x1, other arithmetic, per_device(): keyed = jnp.concatenate([kv_pat, far, anchors], axis=1)  21.3 us
    all_gather x1, waiting for transfers between devices, per_device(): rows_solve = lambda base_x: jnp.sum(lax.all_gather(base_x, 'mp'), axis=0)  19.1 us
    slice x1, local copies, waits for them, and re-layouts, attend_block(): value_part = pairs[:, :, 1, :].reshape(npat, keys, heads, HDIM)  15.1 us
    dot_general x1, matrix products, attend_block(): jnp.einsum('pqhd,pkhd->phqk', query, key_part, preferred_element_type=jnp...  13.9 us
    dot_general x1, matrix products, attend_block(): jnp.einsum('phqk,pkhd->pqhd', weights, value_part, preferred_element_type...  13.5 us
  transfers between devices with their start and end apart: 6, of which 2 were waited for; matrix products, arithmetic and copies ran while one was open for 14% of the time, Pallas kernels for 0%

profile of v1, /device:TPU:0, one launch (start us, length us, event | category | flops | bytes accessed | tf_op | source)
XLA Modules:
  0.0 291.6 jit_solution(17529020316450398031)
XLA Ops:
  6.5 0.8 convert_element_type.32
  7.3 1.9 convert_reduce_fusion
  9.3 0.0 copy-start.3
  9.3 2.4 fusion.9
  11.7 4.7 %copy.11 = bf16[1024,3,512]{0,2,1:T(8,128)(2,1)} copy(bf16[1024,3,512]{2,0,1:T(8,128)(2,1)} %param.8) | data formatting | bytes 6291456 | tf_op args[2]
  16.4 7.6 %fusion.32 = (bf16[1024,3,512]{2,0,1:T(8,128)(2,1)S(1)}, f32[1024,3,512]{2,0,1:T(8,128)}) fusion(bf16[1024,3,512]{0,2,1:T(8,128)(2,1)} %copy.11, bf16[1024,1024]{1,0:T(8,128)(2,1)S(1)} %copy-done.3, f32[1024]{0:T(1024)S(1)} %convert_element_type.32, f32[1024]{0:T(1024)S(1)} %add_rsqrt_fusion, f32[1024]{0:T(1024)S(1)} %broadcast_multiply_fusion), kind=kOutput, calls=%fused_computation.57 | convolution fusion | flops 3228041216 | bytes 14692352 | tf_op jit(solution)/shard_map/dot_general | solution.py:32
  24.0 1.7 copy-done.4
  25.7 0.8 fusion.30
  26.5 3.0 %collective-permute-start.1 = (bf16[2,64,2,512]{3,1,0,2:T(8,128)(2,1)}, bf16[2,64,2,512]{3,1,0,2:T(8,128)(2,1)}, u32[]{:S(2)}, u32[]{:S(2)}) collective-permute-start(bf16[2,64,2,512]{3,1,0,2:T(8,128)(2,1)} %bitcast.6), channel_id=1, source_target_pairs={{28,0},{30,2},{0,4},{2,6},{4,8},{6,10},{8,12},{10,14},{12,16},{14,... | collective-permute-start | bytes 786440 | tf_op jit(solution)/shard_map/ppermute | solution.py:19
  29.5 1.5 collective-permute-start
  31.0 3.2 %collective-permute-start.3 = (bf16[2,64,2,512]{3,1,0,2:T(8,128)(2,1)}, bf16[2,64,2,512]{3,1,0,2:T(8,128)(2,1)S(1)}, u32[]{:S(2)}, u32[]{:S(2)}) collective-permute-start(bf16[2,64,2,512]{3,1,0,2:T(8,128)(2,1)} %bitcast.7), channel_id=1, source_target_pairs={{4,0},{6,2},{8,4},{10,6},{12,8},{14,10},{16,12},{18,14},{20,16},{2... | collective-permute-start | bytes 786440 | tf_op jit(solution)/shard_map/ppermute | solution.py:19
  34.2 1.3 collective-permute-start.2
  35.5 1.6 slice_select_fusion
  37.0 0.0 all-reduce.2.cloned.1.call-update
  37.1 0.0 all-gather.3.cloned.1.call-start
  37.1 1.7 fusion.31
  38.8 0.1 iota_compare_fusion
  38.9 3.5 %fusion.19 = bf16[1024,1,512]{2,0,1:T(8,128)(2,1)} fusion(f32[1024,3,512]{2,0,1:T(8,128)} %get-tuple-element.12), kind=kLoop, calls=%fused_computation.23 | loop fusion | flops 1048576 | bytes 3145728 | tf_op jit(solution)/shard_map/convert_element_type | solution.py:33
  42.4 1.5 maximum_dynamic-update-slice_fusion
  43.9 0.1 broadcast_in_dim.43
  44.0 0.1 reshape.45
  44.1 0.1 pad_add_fusion
  44.2 0.1 copy.12
  44.3 0.1 reshape.49
  44.4 3.0 %convert_element_type.35 = bf16[16,64,8,64]{3,2,1,0:T(8,128)(2,1)S(1)} reshape(bf16[1024,1,512]{2,0,1:T(8,128)(2,1)} %fusion.19) | data formatting | bytes 2097152 | tf_op jit(solution)/shard_map/convert_element_type | solution.py:33
  47.4 1.7 constant_dynamic-update-slice_fusion.3
  49.1 0.0 collective-permute-done.1
  49.1 1.7 constant_dynamic-update-slice_fusion.2
  50.8 1.7 constant_dynamic-update-slice_fusion.1
  52.4 0.0 collective-permute-done.3
  52.4 0.7 constant_dynamic-update-slice_fusion
  53.2 10.2 %gather_fusion = bf16[128,64,2,512]{3,1,2,0:T(8,128)(2,1)} fusion(bf16[24,64,2,512]{3,1,0,2:T(8,128)(2,1)} %constant_dynamic-update-slice_fusion, s32[1024]{0:T(1024)S(1)} %pad_clamp_fusion), kind=kCustom, calls=%fused_computation | custom fusion | bytes 33554944 | tf_op jit(solution)/shard_map/gather | solution.py:95
  63.3 14.2 %copy.13 = bf16[128,64,2,512]{3,1,0,2:T(8,128)(2,1)} copy(bf16[128,64,2,512]{3,1,2,0:T(8,128)(2,1)} %gather_fusion) | data formatting | bytes 33554432 | tf_op jit(solution)/shard_map/gather | solution.py:95
  77.5 65.7 %all-reduce.2.cloned.1.call-done = bf16[64,2,512]{2,0,1:T(8,128)(2,1)} async-done(((bf16[64,2,512]{2,0,1:T(8,128)(2,1)}), bf16[64,2,512]{2,0,1:T(8,128)(2,1)}) %all-reduce.2.cloned.1.call-update) | async-done | bytes 131088 | tf_op jit(solution)/shard_map/psum | solution.py:13
  143.2 2.5 broadcast_in_dim.41
  145.6 21.3 %pad_maximum_fusion = bf16[16,640,2,512]{3,1,0,2:T(8,128)(2,1)} fusion(bf16[16,64,2,512]{3,1,0,2:T(8,128)(2,1)} %broadcast_in_dim.41, bf16[16,512,2,512]{3,1,0,2:T(8,128)(2,1)} %bitcast.36, bf16[16,64,1,512]{3,1,0,2:T(8,128)(2,1)} %bitcast.41, bf16[16,64,1,512]{3,1,0,2:T(8,128)(2,1)} %bitcast.39), kind=kLoop, calls=%fused_computation.1 | loop fusion | flops 83886080 | bytes 41943040 | tf_op jit(solution)/shard_map/concatenate | solution.py:97
  166.9 16.2 %fusion.29 = (bf16[16,640,1,512]{3,1,0,2:T(8,128)(2,1)}, bf16[16,640,1,512]{3,1,0,2:T(8,128)(2,1)}) fusion(bf16[16,640,2,512]{3,1,0,2:T(8,128)(2,1)} %pad_maximum_fusion), kind=kLoop, calls=%fused_computation.54 | loop fusion | bytes 41943040 | tf_op jit(solution)/shard_map/slice | solution.py:42
  183.1 14.7 %copy.15 = bf16[16,640,1,512]{1,3,0,2:T(8,128)(2,1)} copy(bf16[16,640,1,512]{3,1,0,2:T(8,128)(2,1)} %get-tuple-element.5) | data formatting | bytes 20971520 | tf_op jit(solution)/shard_map/slice | solution.py:42
  197.8 15.1 %copy.14 = bf16[16,640,1,512]{1,3,0,2:T(8,128)(2,1)} copy(bf16[16,640,1,512]{3,1,0,2:T(8,128)(2,1)} %get-tuple-element.6) | data formatting | bytes 20971520 | tf_op jit(solution)/shard_map/slice | solution.py:43
  212.9 13.9 %select_reduce_fusion = (f32[16,8,64]{2,1,0:T(8,128)S(1)}, f32[16,8,64,640]{3,2,1,0:T(8,128)}) fusion(pred[16,640]{1,0:T(8,128)(4,1)S(1)} %pad_add_fusion, bf16[16,640,8,64]{1,3,2,0:T(8,128)(2,1)} %bitcast.35, bf16[16,64,8,64]{3,2,1,0:T(8,128)(2,1)S(1)} %convert_element_type.35), kind=kOutput, calls=%fused_computation.3 | convolution fusion | flops 681566208 | bytes 32548864 | tf_op jit(solution)/shard_map/pqhd,pkhd->phqk/dot_general | solution.py:44
  226.8 9.4 %fusion = f32[16,8,64]{2,1,0:T(8,128)S(1)} fusion(f32[16,8,64,640]{3,2,1,0:T(8,128)} %get-tuple-element.14, f32[16,8,64]{2,1,0:T(8,128)S(1)} %get-tuple-element.13, pred[16,640]{1,0:T(8,128)(4,1)S(1)} %pad_add_fusion), kind=kLoop, calls=%fused_computation.4 | loop fusion | flops 15720448 | bytes 21047296 | tf_op jit(solution)/shard_map/reduce_sum | solution.py:48
  236.2 13.5 %fusion.12 = bf16[16,64,8,64]{1,3,2,0:T(8,128)(2,1)} fusion(bf16[16,640,8,64]{1,3,2,0:T(8,128)(2,1)} %bitcast.37, f32[16,8,64,640]{3,2,1,0:T(8,128)} %get-tuple-element.14, f32[16,8,64]{2,1,0:T(8,128)S(1)} %get-tuple-element.13, pred[16,640]{1,0:T(8,128)(4,1)S(1)} %pad_add_fusion, f32[16,64,8]{1,2,0:T(8,128)S(1)} %bitcast.43), kind=kOutput, calls=%fused_computation.18 | convolution fusion | flops 687865856 | bytes 32581632 | tf_op jit(solution)/shard_map/phqk,pkhd->pqhd/dot_general | solution.py:50
  249.8 3.2 %copy.17 = bf16[16,64,8,64]{3,2,1,0:T(8,128)(2,1)S(1)} copy(bf16[16,64,8,64]{1,3,2,0:T(8,128)(2,1)} %fusion.12) | data formatting | bytes 2097152 | tf_op jit(solution)/shard_map/convert_element_type | solution.py:52
  253.0 2.0 reshape.46
  255.1 4.4 %fusion.33 = f32[1024,1024]{1,0:T(8,128)} fusion(bf16[1024,512]{1,0:T(8,128)(2,1)} %reshape.46, bf16[512,1024]{1,0:T(8,128)(2,1)S(1)} %copy-done), kind=kOutput, calls=%fused_computation.58 | convolution fusion | flops 1073741824 | bytes 6291456 | tf_op jit(solution)/shard_map/dot_general | solution.py:103
  259.5 0.0 all-gather.3.cloned.1.call-update
  259.5 19.1 %all-gather.3.cloned.1.call-done = f32[2048,1024]{1,0:T(8,128)} async-done(((f32[1024,1024]{1,0:T(8,128)}), f32[2048,1024]{1,0:T(8,128)}) %all-gather.3.cloned.1.call-update) | async-done | bytes 8388624 | tf_op jit(solution)/shard_map/all_gather | solution.py:104
  278.6 6.2 %reduce_sum.39 = bf16[1024,1024]{1,0:T(8,128)(2,1)} reduce(f32[2,1024,1024]{2,1,0:T(8,128)} %bitcast.42, f32[]{:T(128)} %constant.55.clone.1), dimensions={0}, to_apply=%region_5.6 | reduce | flops 1048576 | bytes 10485764 | tf_op jit(solution)/shard_map/reduce_sum | solution.py:104
  (20 shorter events, 0.1 us)
Async XLA Ops:
  6.5 248.5 %copy-start = (bf16[512,1024]{1,0:T(8,128)(2,1)S(1)}, bf16[512,1024]{1,0:T(8,128)(2,1)}, u32[]{:S(2)}) copy-start(bf16[512,1024]{1,0:T(8,128)(2,1)} %param.9) | copy-start | bytes 3145732
  6.5 136.6 %all-reduce.2.cloned.1.call-start = ((), (), s32[]{:S(2)}) async-start(), calls=%async_computation | async-start | bytes 262144 | tf_op jit(solution)/shard_map/psum | solution.py:13
  9.3 7.2 %copy-start.3 = (bf16[1024,1024]{1,0:T(8,128)(2,1)S(1)}, bf16[1024,1024]{1,0:T(8,128)(2,1)}, u32[]{:S(2)}) copy-start(bf16[1024,1024]{1,0:T(8,128)(2,1)} %param.6) | copy-start | bytes 6291460
  24.0 1.7 copy-start.4
  24.0 14.8 %copy-start.6 = (s32[16]{0:T(128)S(1)}, s32[16]{0:T(128)}, u32[]{:S(2)}) copy-start(s32[16]{0:T(128)} %param.11) | copy-start | bytes 196
  24.0 14.9 %copy-start.5 = (s32[16,8]{0,1:T(8,128)S(1)}, s32[16,8]{0,1:T(8,128)}, u32[]{:S(2)}) copy-start(s32[16,8]{0,1:T(8,128)} %param.10) | copy-start | bytes 1540
  26.5 22.6 %collective-permute-start.1 = (bf16[2,64,2,512]{3,1,0,2:T(8,128)(2,1)}, bf16[2,64,2,512]{3,1,0,2:T(8,128)(2,1)}, u32[]{:S(2)}, u32[]{:S(2)}) collective-permute-start(bf16[2,64,2,512]{3,1,0,2:T(8,128)(2,1)} %bitcast.6), channel_id=1, source_target_pairs={{28,0},{30,2},{0,4},{2,6},{4,8},{6,10},{8,12},{10,14},{12,16},{14,... | collective-permute-start | bytes 786440 | tf_op jit(solution)/shard_map/ppermute | solution.py:19
  29.5 17.9 %collective-permute-start = (bf16[2,64,2,512]{3,1,0,2:T(8,128)(2,1)}, bf16[2,64,2,512]{3,1,0,2:T(8,128)(2,1)}, u32[]{:S(2)}, u32[]{:S(2)}) collective-permute-start(bf16[2,64,2,512]{3,1,0,2:T(8,128)(2,1)} %bitcast.6), channel_id=1, source_target_pairs={{30,0},{0,2},{2,4},{4,6},{6,8},{8,10},{10,12},{12,14},{14,16},{16,... | collective-permute-start | bytes 786440 | tf_op jit(solution)/shard_map/ppermute | solution.py:19
  31.0 21.5 %collective-permute-start.3 = (bf16[2,64,2,512]{3,1,0,2:T(8,128)(2,1)}, bf16[2,64,2,512]{3,1,0,2:T(8,128)(2,1)S(1)}, u32[]{:S(2)}, u32[]{:S(2)}) collective-permute-start(bf16[2,64,2,512]{3,1,0,2:T(8,128)(2,1)} %bitcast.7), channel_id=1, source_target_pairs={{4,0},{6,2},{8,4},{10,6},{12,8},{14,10},{16,12},{18,14},{20,16},{2... | collective-permute-start | bytes 786440 | tf_op jit(solution)/shard_map/ppermute | solution.py:19
  34.2 16.6 %collective-permute-start.2 = (bf16[2,64,2,512]{3,1,0,2:T(8,128)(2,1)}, bf16[2,64,2,512]{3,1,0,2:T(8,128)(2,1)}, u32[]{:S(2)}, u32[]{:S(2)}) collective-permute-start(bf16[2,64,2,512]{3,1,0,2:T(8,128)(2,1)} %bitcast.7), channel_id=1, source_target_pairs={{2,0},{4,2},{6,4},{8,6},{10,8},{12,10},{14,12},{16,14},{18,16},{20... | collective-permute-start | bytes 786440 | tf_op jit(solution)/shard_map/ppermute | solution.py:19
  37.1 241.5 %all-gather.3.cloned.1.call-start = ((), (), s32[]{:S(2)}) async-start(), calls=%async_computation.1 | async-start | bytes 12582912 | tf_op jit(solution)/shard_map/all_gather | solution.py:104
  38.8 3.6 %copy-start.1 = (bf16[1024,1,512]{2,0,1:T(8,128)(2,1)}, bf16[1024,1,512]{2,0,1:T(8,128)(2,1)S(1)}, u32[]{:S(2)}) copy-start(bf16[1024,1,512]{2,0,1:T(8,128)(2,1)S(1)} %get-tuple-element.9) | copy-start | bytes 3145732
  38.8 5.1 %copy-start.2 = (bf16[1024,1,512]{2,0,1:T(8,128)(2,1)}, bf16[1024,1,512]{2,0,1:T(8,128)(2,1)S(1)}, u32[]{:S(2)}) copy-start(bf16[1024,1,512]{2,0,1:T(8,128)(2,1)S(1)} %get-tuple-element.10) | copy-start | bytes 3145732
Sparse Core Ops, SparseCore 0:
  37.2 105.9 all-reduce.1
  259.6 18.8 all-gather.2
